TPU v7x, 32 devices: a whole 2x2x4 slice. The times are simulated.
32 devices in a mesh: gx: 2 (over x), gy: 4 (over z), gz: 4 (over y, core).
Axes of the slice: x: 2, y: 2, z: 4, core: 2. Of those that a mesh axis runs over, the one named last changes fastest.
Arguments:
- local_displacement: float32 [2, 4, 4, 6, 128, 128], P('gx', 'gy', 'gz'), may hold values from -6 to 6
- coarse_load: float32 [2, 4, 4, 6, 128], P('gx', 'gy', 'gz'), may hold values from -12 to 12
- flexibility: float32 [2, 4, 4, 768, 768], P('gx', 'gy', 'gz'), as said below
- block_map: int32 [2, 4, 4, 768], P('gx', 'gy', 'gz'), may hold values from 0 to 767, each once within a row
- mode_counts: int32 [2, 4, 4], P('gx', 'gy', 'gz'), may hold values from 3 to 6, as said below
- mode_traces: float32 [2, 4, 4, 6, 6, 128], P('gx', 'gy', 'gz')
- coarse_rows: float32 [2, 4, 4, 6, 192], P('gx', 'gy', 'gz'), as said below
- stored_dirs: float32 [2, 4, 4, 40, 6, 128], P('gx', 'gy', 'gz'), as said below
- stored_images: float32 [2, 4, 4, 40, 6, 128], P('gx', 'gy', 'gz'), as said below
- stored_curv: float32 [40], replicated, may hold values from 1 to 4
Outputs:
- multipliers: float32 [2, 4, 4, 6, 128, 128], P('gx', 'gy', 'gz')
- residual: float32 [2, 4, 4, 6, 128, 128], P('gx', 'gy', 'gz')
Inputs may be any that keep to these rules, and one draw needn't show every extreme that they name: `flexibility`: each subdomain's matrix is symmetric positive definite. `coarse_rows`: read as a [192, 192] matrix it is exactly symmetric: the inverse of G^T G for the coarse basis G of the present modes, with ones added on the diagonal of absent modes. `mode_counts`: modes numbered from the count on are absent. `block_map`: each subdomain's row names every interface position once. `stored_dirs`: both copies of every face agree: slot 2a of a subdomain equals slot 2a+1 of its lower neighbour along grid dimension a. `stored_images`: both copies of every face agree: slot 2a of a subdomain equals slot 2a+1 of its lower neighbour along grid dimension a.
All inputs are finite; a program needn't handle non-finite values.
Results may differ from a plain program's by a relative error of at most 0.0003.
Values sent between devices are 32-bit elements; how exact they have to be, the bound alone decides.
A program may use at most 128 MiB of HBM per device.

v0:
```python
import jax
import jax.numpy as jnp
from jax import lax
from jax.sharding import PartitionSpec as P

STORED = 40
ITERS = 3
precise = lax.Precision.HIGHEST
slot_signs = (-1.0, 1.0, -1.0, 1.0, -1.0, 1.0)


def extended(x, sides, width):
    for axis, dim in sides:
        peers, length = (lax.axis_size(axis), x.shape[dim])
        up = [(i, (i + 1) % peers) for i in range(peers)]
        down = [(j, i) for i, j in up]
        last = lax.slice_in_dim(x, length - width, length, axis=dim)
        initial = lax.slice_in_dim(x, 0, width, axis=dim)
        before = lax.ppermute(last, axis, up)
        after = lax.ppermute(initial, axis, down)
        x = jnp.concatenate([before, x, after], axis=dim)
    return x


def assemble(field):
    padded_x = extended(field[0:2], (("gx", 0),), 1)
    padded_y = extended(field[2:4], (("gy", 0),), 1)
    padded_z = extended(field[4:6], (("gz", 0),), 1)
    return jnp.stack(
        [
            field[0] + padded_x[0],
            field[1] + padded_x[3],
            field[2] + padded_y[0],
            field[3] + padded_y[3],
            field[4] + padded_z[0],
            field[5] + padded_z[3],
        ]
    )


def plus_inner(first, second):
    return jnp.sum(first[1::2] * second[1::2], axis=(0, 1))


def stored_inner(store, field):
    return jnp.einsum("isf,sfr->ir", store[:, 1::2], field[1::2], precision=precise)


def coarse_solve(loads, rows):
    return jnp.dot(
        rows, lax.all_gather(loads, ("gx", "gy", "gz"), axis=0, tiled=True), precision=precise
    )


def per_device(
    local_displacement,
    coarse_load,
    flexibility,
    block_map,
    mode_counts,
    mode_traces,
    coarse_rows,
    stored_dirs,
    stored_images,
    stored_curv,
):
    displacement = local_displacement[0, 0, 0]
    loads = coarse_load[0, 0, 0]
    flex = flexibility[0, 0, 0]
    mapping = block_map[0, 0, 0]
    rows = coarse_rows[0, 0, 0]
    dirs_store = stored_dirs[0, 0, 0]
    images_store = stored_images[0, 0, 0]
    signs = jnp.array(slot_signs, jnp.float32)
    field_signs = signs[:, None, None]
    nmodes = mode_traces.shape[3]
    present = (jnp.arange(nmodes, dtype=jnp.int32) < mode_counts[0, 0, 0]).astype(jnp.float32)
    signed = mode_traces[0, 0, 0] * present[:, None, None] * signs[None, :, None]
    size_nb = flex.shape[0]
    inverse = jnp.zeros((size_nb,), jnp.int32).at[mapping].set(jnp.arange(size_nb, dtype=jnp.int32))
    flex_face = jnp.take(jnp.take(flex, inverse, axis=0), inverse, axis=1)
    layout = displacement.shape

    def operate(field):
        flat = (field_signs * field).reshape(size_nb, layout[2])
        return jnp.dot(flex_face, flat, precision=precise).reshape(layout)

    def graph(alpha):
        return assemble(jnp.einsum("msf,mr->sfr", signed, alpha, precision=precise))

    def project(field):
        partial_loads = jnp.einsum("msf,sfr->mr", signed, field, precision=precise)
        return field - graph(coarse_solve(partial_loads, rows))

    lam = graph(coarse_solve(loads, rows))
    resid = project(assemble(field_signs * (displacement - operate(lam))))
    directions, images, curves = ([], [], [])
    for step in range(ITERS):
        local_rows = stored_inner(images_store, resid)
        if images:
            own_rows = jnp.stack([plus_inner(images[index], resid) for index in range(len(images))])
            local_rows = jnp.concatenate([local_rows, own_rows], axis=0)
        totals = lax.psum(local_rows, ("gx", "gy", "gz"))
        beta = totals[:STORED] / stored_curv[:, None]
        direction = resid - jnp.einsum("isf,ir->sfr", dirs_store, beta, precision=precise)
        for index in range(len(directions)):
            direction = direction - directions[index] * (totals[STORED + index] / curves[index])
        image_now = project(assemble(field_signs * operate(direction)))
        pair = lax.psum(
            jnp.stack([plus_inner(direction, image_now), plus_inner(direction, resid)]),
            ("gx", "gy", "gz"),
        )
        rate = pair[1] / pair[0]
        lam = lam + rate * direction
        resid = resid - rate * image_now
        directions.append(direction)
        images.append(image_now)
        curves.append(pair[0])
    return (lam[None, None, None], resid[None, None, None])


def solution(mesh):
    return jax.shard_map(
        per_device,
        mesh=mesh,
        in_specs=(
            P("gx", "gy", "gz", None, None, None),
            P("gx", "gy", "gz", None, None),
            P("gx", "gy", "gz", None, None),
            P("gx", "gy", "gz", None),
            P("gx", "gy", "gz"),
            P("gx", "gy", "gz", None, None, None),
            P("gx", "gy", "gz", None, None),
            P("gx", "gy", "gz", None, None, None),
            P("gx", "gy", "gz", None, None, None),
            P(),
        ),
        out_specs=(P("gx", "gy", "gz", None, None, None), P("gx", "gy", "gz", None, None, None)),
        check_vma=False,
    )
```

profile of v0, /device:TPU:10, one launch (start us, length us, event | category | flops | bytes accessed | tf_op | source)
XLA Modules:
  0.0 665.6 jit_solution(9631356648595068276)
XLA Ops:
  1.5 37.6 %all-gather = f32[1,1,1,192,128]{4,2,1,0,3:T(1,128)S(1)} all-gather(f32[1,1,1,6,128]{4,2,1,0,3:T(1,128)} %bitcast.275), channel_id=2, replica_groups=mesh['gx'=2,'gy'=4,'gz'=4] {'gx','gy','gz'}, dimensions={3}, use_global_device_ids=true | all-gather | bytes 101376 | tf_op jit(solution)/shard_map/all_gather | solution.py:51
  43.9 3.4 scatter_custom_fusion
  47.3 3.5 gather_fusion
  57.1 5.8 gather_fusion.1
  71.2 4.2 collective-permute-start.3
  78.9 3.7 fusion.4
  87.5 4.6 collective-permute-start.8
  99.1 37.6 %all-gather.1 = f32[32,6,128]{2,1,0:T(8,128)S(1)} all-gather(f32[1,6,128]{2,1,0:T(8,128)S(1)} %convolution_bitcast_fusion.14), channel_id=1, replica_groups=mesh['gx'=2,'gy'=4,'gz'=4] {'gx','gy','gz'}, dimensions={0}, use_global_device_ids=true | all-gather | bytes 101376 | tf_op jit(solution)/shard_map/all_gather | solution.py:51
  142.8 4.2 collective-permute-start.15
  153.1 43.5 %psum.42 = f32[40,128]{1,0:T(8,128)} all-reduce(f32[40,128]{1,0:T(8,128)S(1)} %convolution_bitcast_fusion.5), channel_id=1, replica_groups=mesh['gx'=2,'gy'=4,'gz'=4] {'gx','gy','gz'}, use_global_device_ids=true, to_apply=%region_1.2 | all-reduce | flops 5120 | bytes 40960 | tf_op jit(solution)/shard_map/psum | solution.py:103
  198.4 3.7 convolution_multiply_fusion.2
  202.4 4.1 collective-permute-done.18
  209.7 3.6 collective-permute-done.19
  214.1 39.5 %all-gather.2 = f32[32,6,128]{2,1,0:T(8,128)} all-gather(f32[1,6,128]{2,1,0:T(8,128)S(1)} %convolution_bitcast_fusion.13), channel_id=1, replica_groups=mesh['gx'=2,'gy'=4,'gz'=4] {'gx','gy','gz'}, dimensions={0}, use_global_device_ids=true | all-gather | bytes 101376 | tf_op jit(solution)/shard_map/all_gather | solution.py:51
  267.2 4.2 collective-permute-start.27
  272.8 3.4 collective-permute-done.25
  278.5 42.5 %psum.43 = f32[2,128]{1,0:T(2,128)S(1)} all-reduce(f32[2,128]{1,0:T(2,128)S(1)} %pad_maximum_fusion.2), channel_id=1, replica_groups=mesh['gx'=2,'gy'=4,'gz'=4] {'gx','gy','gz'}, use_global_device_ids=true, to_apply=%region_4.5 | all-reduce | flops 256 | bytes 2048 | tf_op jit(solution)/shard_map/psum | solution.py:109
  324.6 39.2 %psum.44 = f32[41,128]{1,0:T(8,128)S(1)} all-reduce(f32[41,128]{1,0:T(8,128)S(1)} %pad_maximum_fusion), channel_id=1, replica_groups=mesh['gx'=2,'gy'=4,'gz'=4] {'gx','gy','gz'}, use_global_device_ids=true, to_apply=%region_6.7 | all-reduce | flops 5248 | bytes 41984 | tf_op jit(solution)/shard_map/psum | solution.py:103
  367.1 3.7 convolution_multiply_fusion.1
  371.0 4.1 collective-permute-done.30
  378.5 3.9 collective-permute-done.31
  383.3 38.7 %all-gather.3 = f32[32,6,128]{2,1,0:T(8,128)S(1)} all-gather(f32[1,6,128]{2,1,0:T(8,128)S(1)} %convolution_bitcast_fusion.12), channel_id=1, replica_groups=mesh['gx'=2,'gy'=4,'gz'=4] {'gx','gy','gz'}, dimensions={0}, use_global_device_ids=true | all-gather | bytes 101376 | tf_op jit(solution)/shard_map/all_gather | solution.py:51
  433.3 4.2 collective-permute-start.39
  438.8 3.6 collective-permute-done.37
  445.1 42.5 %psum.45 = f32[2,128]{1,0:T(2,128)} all-reduce(f32[2,128]{1,0:T(2,128)} %pad_maximum_fusion.3), channel_id=1, replica_groups=mesh['gx'=2,'gy'=4,'gz'=4] {'gx','gy','gz'}, use_global_device_ids=true, to_apply=%region_9.10 | all-reduce | flops 256 | bytes 2048 | tf_op jit(solution)/shard_map/psum | solution.py:109
  491.8 39.6 %psum.46 = f32[42,128]{1,0:T(8,128)S(1)} all-reduce(f32[42,128]{1,0:T(8,128)S(1)} %pad_maximum_fusion.1), channel_id=1, replica_groups=mesh['gx'=2,'gy'=4,'gz'=4] {'gx','gy','gz'}, use_global_device_ids=true, to_apply=%region_12.13 | all-reduce | flops 5376 | bytes 43008 | tf_op jit(solution)/shard_map/psum | solution.py:103
  534.9 3.7 convolution_multiply_fusion
  538.9 4.1 collective-permute-done.42
  546.3 3.6 collective-permute-done.43
  550.9 38.9 %all-gather.4 = f32[32,6,128]{2,1,0:T(8,128)S(1)} all-gather(f32[1,6,128]{2,1,0:T(8,128)S(1)} %convolution_bitcast_fusion.11), channel_id=1, replica_groups=mesh['gx'=2,'gy'=4,'gz'=4] {'gx','gy','gz'}, dimensions={0}, use_global_device_ids=true | all-gather | bytes 101376 | tf_op jit(solution)/shard_map/all_gather | solution.py:51
  601.0 4.2 collective-permute-start.51
  611.6 42.5 %psum.47 = f32[2,128]{1,0:T(2,128)S(1)} all-reduce(f32[2,128]{1,0:T(2,128)S(1)} %pad_maximum_fusion.4), channel_id=1, replica_groups=mesh['gx'=2,'gy'=4,'gz'=4] {'gx','gy','gz'}, use_global_device_ids=true, to_apply=%region_15.16 | all-reduce | flops 256 | bytes 2048 | tf_op jit(solution)/shard_map/psum | solution.py:109
  (456 shorter events, 137.0 us)
Async XLA Ops:
  41.6 21.3 %collective-permute-start = (f32[1,128,128]{2,1,0:T(8,128)S(1)}, f32[1,128,128]{2,1,0:T(8,128)}, u32[]{:S(2)}, u32[]{:S(2)}) collective-permute-start(f32[1,128,128]{2,1,0:T(8,128)S(1)} %slice.456), channel_id=1, source_target_pairs={{0,16},{16,0},{1,17},{17,1},{2,18},{18,2},{3,19},{19,3},{4,20},{20... | collective-permute-start | bytes 196616 | tf_op jit(solution)/shard_map/ppermute | solution.py:19
  63.7 11.7 %collective-permute-start.1 = (f32[1,128,128]{2,1,0:T(8,128)S(1)}, f32[1,128,128]{2,1,0:T(8,128)}, u32[]{:S(2)}, u32[]{:S(2)}) collective-permute-start(f32[1,128,128]{2,1,0:T(8,128)S(1)} %get-tuple-element.63), channel_id=1, source_target_pairs={{16,0},{0,16},{17,1},{1,17},{18,2},{2,18},{19,3},{3,19},{20,4},{4,... | collective-permute-start | bytes 196616 | tf_op jit(solution)/shard_map/ppermute | solution.py:20
  70.7 7.4 %collective-permute-start.5 = (f32[1,128,128]{2,1,0:T(8,128)S(1)}, f32[1,128,128]{2,1,0:T(8,128)S(1)}, u32[]{:S(2)}, u32[]{:S(2)}) collective-permute-start(f32[1,128,128]{2,1,0:T(8,128)S(1)} %get-tuple-element.58), channel_id=1, source_target_pairs={{1,0},{2,1},{3,2},{0,3},{5,4},{6,5},{7,6},{4,7},{9,8},{10,9},{11,1... | collective-permute-start | bytes 196616 | tf_op jit(solution)/shard_map/ppermute | solution.py:20
  70.7 7.3 %collective-permute-start.4 = (f32[1,128,128]{2,1,0:T(8,128)S(1)}, f32[1,128,128]{2,1,0:T(8,128)S(1)}, u32[]{:S(2)}, u32[]{:S(2)}) collective-permute-start(f32[1,128,128]{2,1,0:T(8,128)S(1)} %get-tuple-element.60), channel_id=1, source_target_pairs={{0,1},{1,2},{2,3},{3,0},{4,5},{5,6},{6,7},{7,4},{8,9},{9,10},{10,1... | collective-permute-start | bytes 196616 | tf_op jit(solution)/shard_map/ppermute | solution.py:19
  87.0 11.1 %collective-permute-start.11 = (f32[1,128,128]{2,1,0:T(8,128)S(1)}, f32[1,128,128]{2,1,0:T(8,128)S(1)}, u32[]{:S(2)}, u32[]{:S(2)}) collective-permute-start(f32[1,128,128]{2,1,0:T(8,128)S(1)} %get-tuple-element.52), channel_id=1, source_target_pairs={{1,0},{2,1},{3,2},{0,3},{5,4},{6,5},{7,6},{4,7},{9,8},{10,9},{11,1... | collective-permute-start | bytes 196616 | tf_op jit(solution)/shard_map/ppermute | solution.py:20
  87.0 11.0 %collective-permute-start.10 = (f32[1,128,128]{2,1,0:T(8,128)S(1)}, f32[1,128,128]{2,1,0:T(8,128)S(1)}, u32[]{:S(2)}, u32[]{:S(2)}) collective-permute-start(f32[1,128,128]{2,1,0:T(8,128)S(1)} %get-tuple-element.54), channel_id=1, source_target_pairs={{0,1},{1,2},{2,3},{3,0},{4,5},{5,6},{6,7},{7,4},{8,9},{9,10},{10,1... | collective-permute-start | bytes 196616 | tf_op jit(solution)/shard_map/ppermute | solution.py:19
  87.5 8.9 %collective-permute-start.8 = (f32[1,128,128]{2,1,0:T(8,128)S(1)}, f32[1,128,128]{2,1,0:T(8,128)S(1)}, u32[]{:S(2)}, u32[]{:S(2)}) collective-permute-start(f32[1,128,128]{2,1,0:T(8,128)S(1)} %get-tuple-element.55), channel_id=1, source_target_pairs={{0,4},{4,8},{8,12},{12,0},{1,5},{5,9},{9,13},{13,1},{2,6},{6,10},{... | collective-permute-start | bytes 196616 | tf_op jit(solution)/shard_map/ppermute | solution.py:19
  142.2 9.3 %collective-permute-start.17 = (f32[1,128,128]{2,1,0:T(8,128)S(1)}, f32[1,128,128]{2,1,0:T(8,128)S(1)}, u32[]{:S(2)}, u32[]{:S(2)}) collective-permute-start(f32[1,128,128]{2,1,0:T(8,128)S(1)} %get-tuple-element.46), channel_id=1, source_target_pairs={{1,0},{2,1},{3,2},{0,3},{5,4},{6,5},{7,6},{4,7},{9,8},{10,9},{11,1... | collective-permute-start | bytes 196616 | tf_op jit(solution)/shard_map/ppermute | solution.py:20
  142.3 9.2 %collective-permute-start.16 = (f32[1,128,128]{2,1,0:T(8,128)S(1)}, f32[1,128,128]{2,1,0:T(8,128)S(1)}, u32[]{:S(2)}, u32[]{:S(2)}) collective-permute-start(f32[1,128,128]{2,1,0:T(8,128)S(1)} %get-tuple-element.48), channel_id=1, source_target_pairs={{0,1},{1,2},{2,3},{3,0},{4,5},{5,6},{6,7},{7,4},{8,9},{9,10},{10,1... | collective-permute-start | bytes 196616 | tf_op jit(solution)/shard_map/ppermute | solution.py:19
  142.8 8.6 %collective-permute-start.14 = (f32[1,128,128]{2,1,0:T(8,128)S(1)}, f32[1,128,128]{2,1,0:T(8,128)S(1)}, u32[]{:S(2)}, u32[]{:S(2)}) collective-permute-start(f32[1,128,128]{2,1,0:T(8,128)S(1)} %get-tuple-element.49), channel_id=1, source_target_pairs={{0,4},{4,8},{8,12},{12,0},{1,5},{5,9},{9,13},{13,1},{2,6},{6,10},{... | collective-permute-start | bytes 196616 | tf_op jit(solution)/shard_map/ppermute | solution.py:19
  142.8 8.7 %collective-permute-start.15 = (f32[1,128,128]{2,1,0:T(8,128)S(1)}, f32[1,128,128]{2,1,0:T(8,128)S(1)}, u32[]{:S(2)}, u32[]{:S(2)}) collective-permute-start(f32[1,128,128]{2,1,0:T(8,128)S(1)} %get-tuple-element.50), channel_id=1, source_target_pairs={{4,0},{8,4},{12,8},{0,12},{5,1},{9,5},{13,9},{1,13},{6,2},{10,6},{... | collective-permute-start | bytes 196616 | tf_op jit(solution)/shard_map/ppermute | solution.py:20
  206.5 7.0 %collective-permute-start.23 = (f32[1,128,128]{2,1,0:T(8,128)S(1)}, f32[1,128,128]{2,1,0:T(8,128)S(1)}, u32[]{:S(2)}, u32[]{:S(2)}) collective-permute-start(f32[1,128,128]{2,1,0:T(8,128)S(1)} %get-tuple-element.40), channel_id=1, source_target_pairs={{1,0},{2,1},{3,2},{0,3},{5,4},{6,5},{7,6},{4,7},{9,8},{10,9},{11,1... | collective-permute-start | bytes 196616 | tf_op jit(solution)/shard_map/ppermute | solution.py:20
  206.6 6.9 %collective-permute-start.22 = (f32[1,128,128]{2,1,0:T(8,128)S(1)}, f32[1,128,128]{2,1,0:T(8,128)S(1)}, u32[]{:S(2)}, u32[]{:S(2)}) collective-permute-start(f32[1,128,128]{2,1,0:T(8,128)S(1)} %get-tuple-element.42), channel_id=1, source_target_pairs={{0,1},{1,2},{2,3},{3,0},{4,5},{5,6},{6,7},{7,4},{8,9},{9,10},{10,1... | collective-permute-start | bytes 196616 | tf_op jit(solution)/shard_map/ppermute | solution.py:19
  257.8 8.7 %collective-permute-start.24 = (f32[1,128,128]{2,1,0:T(8,128)S(1)}, f32[1,128,128]{2,1,0:T(8,128)S(1)}, u32[]{:S(2)}, u32[]{:S(2)}) collective-permute-start(f32[1,128,128]{2,1,0:T(8,128)S(1)} %slice.480), channel_id=1, source_target_pairs={{0,16},{16,0},{1,17},{17,1},{2,18},{18,2},{3,19},{19,3},{4,20},{20... | collective-permute-start | bytes 196616 | tf_op jit(solution)/shard_map/ppermute | solution.py:19
  266.6 9.8 %collective-permute-start.29 = (f32[1,128,128]{2,1,0:T(8,128)S(1)}, f32[1,128,128]{2,1,0:T(8,128)S(1)}, u32[]{:S(2)}, u32[]{:S(2)}) collective-permute-start(f32[1,128,128]{2,1,0:T(8,128)S(1)} %get-tuple-element.34), channel_id=1, source_target_pairs={{1,0},{2,1},{3,2},{0,3},{5,4},{6,5},{7,6},{4,7},{9,8},{10,9},{11,1... | collective-permute-start | bytes 196616 | tf_op jit(solution)/shard_map/ppermute | solution.py:20
  266.7 9.7 %collective-permute-start.28 = (f32[1,128,128]{2,1,0:T(8,128)S(1)}, f32[1,128,128]{2,1,0:T(8,128)S(1)}, u32[]{:S(2)}, u32[]{:S(2)}) collective-permute-start(f32[1,128,128]{2,1,0:T(8,128)S(1)} %get-tuple-element.36), channel_id=1, source_target_pairs={{0,1},{1,2},{2,3},{3,0},{4,5},{5,6},{6,7},{7,4},{8,9},{9,10},{10,1... | collective-permute-start | bytes 196616 | tf_op jit(solution)/shard_map/ppermute | solution.py:19
  267.1 9.1 %collective-permute-start.26 = (f32[1,128,128]{2,1,0:T(8,128)S(1)}, f32[1,128,128]{2,1,0:T(8,128)S(1)}, u32[]{:S(2)}, u32[]{:S(2)}) collective-permute-start(f32[1,128,128]{2,1,0:T(8,128)S(1)} %get-tuple-element.37), channel_id=1, source_target_pairs={{0,4},{4,8},{8,12},{12,0},{1,5},{5,9},{9,13},{13,1},{2,6},{6,10},{... | collective-permute-start | bytes 196616 | tf_op jit(solution)/shard_map/ppermute | solution.py:19
  267.2 9.1 %collective-permute-start.27 = (f32[1,128,128]{2,1,0:T(8,128)S(1)}, f32[1,128,128]{2,1,0:T(8,128)S(1)}, u32[]{:S(2)}, u32[]{:S(2)}) collective-permute-start(f32[1,128,128]{2,1,0:T(8,128)S(1)} %get-tuple-element.38), channel_id=1, source_target_pairs={{4,0},{8,4},{12,8},{0,12},{5,1},{9,5},{13,9},{1,13},{6,2},{10,6},{... | collective-permute-start | bytes 196616 | tf_op jit(solution)/shard_map/ppermute | solution.py:20
  375.2 7.3 %collective-permute-start.35 = (f32[1,128,128]{2,1,0:T(8,128)S(1)}, f32[1,128,128]{2,1,0:T(8,128)S(1)}, u32[]{:S(2)}, u32[]{:S(2)}) collective-permute-start(f32[1,128,128]{2,1,0:T(8,128)S(1)} %get-tuple-element.28), channel_id=1, source_target_pairs={{1,0},{2,1},{3,2},{0,3},{5,4},{6,5},{7,6},{4,7},{9,8},{10,9},{11,1... | collective-permute-start | bytes 196616 | tf_op jit(solution)/shard_map/ppermute | solution.py:20
  375.2 7.2 %collective-permute-start.34 = (f32[1,128,128]{2,1,0:T(8,128)S(1)}, f32[1,128,128]{2,1,0:T(8,128)S(1)}, u32[]{:S(2)}, u32[]{:S(2)}) collective-permute-start(f32[1,128,128]{2,1,0:T(8,128)S(1)} %get-tuple-element.30), channel_id=1, source_target_pairs={{0,1},{1,2},{2,3},{3,0},{4,5},{5,6},{6,7},{7,4},{8,9},{9,10},{10,1... | collective-permute-start | bytes 196616 | tf_op jit(solution)/shard_map/ppermute | solution.py:19
  423.8 8.9 %collective-permute-start.36 = (f32[1,128,128]{2,1,0:T(8,128)S(1)}, f32[1,128,128]{2,1,0:T(8,128)S(1)}, u32[]{:S(2)}, u32[]{:S(2)}) collective-permute-start(f32[1,128,128]{2,1,0:T(8,128)S(1)} %slice.494), channel_id=1, source_target_pairs={{0,16},{16,0},{1,17},{17,1},{2,18},{18,2},{3,19},{19,3},{4,20},{20... | collective-permute-start | bytes 196616 | tf_op jit(solution)/shard_map/ppermute | solution.py:19
  432.7 9.8 %collective-permute-start.41 = (f32[1,128,128]{2,1,0:T(8,128)S(1)}, f32[1,128,128]{2,1,0:T(8,128)S(1)}, u32[]{:S(2)}, u32[]{:S(2)}) collective-permute-start(f32[1,128,128]{2,1,0:T(8,128)S(1)} %get-tuple-element.22), channel_id=1, source_target_pairs={{1,0},{2,1},{3,2},{0,3},{5,4},{6,5},{7,6},{4,7},{9,8},{10,9},{11,1... | collective-permute-start | bytes 196616 | tf_op jit(solution)/shard_map/ppermute | solution.py:20
  432.8 9.7 %collective-permute-start.40 = (f32[1,128,128]{2,1,0:T(8,128)S(1)}, f32[1,128,128]{2,1,0:T(8,128)S(1)}, u32[]{:S(2)}, u32[]{:S(2)}) collective-permute-start(f32[1,128,128]{2,1,0:T(8,128)S(1)} %get-tuple-element.24), channel_id=1, source_target_pairs={{0,1},{1,2},{2,3},{3,0},{4,5},{5,6},{6,7},{7,4},{8,9},{9,10},{10,1... | collective-permute-start | bytes 196616 | tf_op jit(solution)/shard_map/ppermute | solution.py:19
  433.3 9.1 %collective-permute-start.38 = (f32[1,128,128]{2,1,0:T(8,128)S(1)}, f32[1,128,128]{2,1,0:T(8,128)S(1)}, u32[]{:S(2)}, u32[]{:S(2)}) collective-permute-start(f32[1,128,128]{2,1,0:T(8,128)S(1)} %get-tuple-element.25), channel_id=1, source_target_pairs={{0,4},{4,8},{8,12},{12,0},{1,5},{5,9},{9,13},{13,1},{2,6},{6,10},{... | collective-permute-start | bytes 196616 | tf_op jit(solution)/shard_map/ppermute | solution.py:19
  433.3 9.1 %collective-permute-start.39 = (f32[1,128,128]{2,1,0:T(8,128)S(1)}, f32[1,128,128]{2,1,0:T(8,128)S(1)}, u32[]{:S(2)}, u32[]{:S(2)}) collective-permute-start(f32[1,128,128]{2,1,0:T(8,128)S(1)} %get-tuple-element.26), channel_id=1, source_target_pairs={{4,0},{8,4},{12,8},{0,12},{5,1},{9,5},{13,9},{1,13},{6,2},{10,6},{... | collective-permute-start | bytes 196616 | tf_op jit(solution)/shard_map/ppermute | solution.py:20
  543.0 7.1 %collective-permute-start.47 = (f32[1,128,128]{2,1,0:T(8,128)S(1)}, f32[1,128,128]{2,1,0:T(8,128)S(1)}, u32[]{:S(2)}, u32[]{:S(2)}) collective-permute-start(f32[1,128,128]{2,1,0:T(8,128)S(1)} %get-tuple-element.16), channel_id=1, source_target_pairs={{1,0},{2,1},{3,2},{0,3},{5,4},{6,5},{7,6},{4,7},{9,8},{10,9},{11,1... | collective-permute-start | bytes 196616 | tf_op jit(solution)/shard_map/ppermute | solution.py:20
  543.1 7.0 %collective-permute-start.46 = (f32[1,128,128]{2,1,0:T(8,128)S(1)}, f32[1,128,128]{2,1,0:T(8,128)S(1)}, u32[]{:S(2)}, u32[]{:S(2)}) collective-permute-start(f32[1,128,128]{2,1,0:T(8,128)S(1)} %get-tuple-element.18), channel_id=1, source_target_pairs={{0,1},{1,2},{2,3},{3,0},{4,5},{5,6},{6,7},{7,4},{8,9},{9,10},{10,1... | collective-permute-start | bytes 196616 | tf_op jit(solution)/shard_map/ppermute | solution.py:19
  591.7 8.7 %collective-permute-start.48 = (f32[1,128,128]{2,1,0:T(8,128)S(1)}, f32[1,128,128]{2,1,0:T(8,128)S(1)}, u32[]{:S(2)}, u32[]{:S(2)}) collective-permute-start(f32[1,128,128]{2,1,0:T(8,128)S(1)} %slice.509), channel_id=1, source_target_pairs={{0,16},{16,0},{1,17},{17,1},{2,18},{18,2},{3,19},{19,3},{4,20},{20... | collective-permute-start | bytes 196616 | tf_op jit(solution)/shard_map/ppermute | solution.py:19
  600.4 9.8 %collective-permute-start.53 = (f32[1,128,128]{2,1,0:T(8,128)S(1)}, f32[1,128,128]{2,1,0:T(8,128)S(1)}, u32[]{:S(2)}, u32[]{:S(2)}) collective-permute-start(f32[1,128,128]{2,1,0:T(8,128)S(1)} %get-tuple-element.10), channel_id=1, source_target_pairs={{1,0},{2,1},{3,2},{0,3},{5,4},{6,5},{7,6},{4,7},{9,8},{10,9},{11,1... | collective-permute-start | bytes 196616 | tf_op jit(solution)/shard_map/ppermute | solution.py:20
  600.5 9.7 %collective-permute-start.52 = (f32[1,128,128]{2,1,0:T(8,128)S(1)}, f32[1,128,128]{2,1,0:T(8,128)S(1)}, u32[]{:S(2)}, u32[]{:S(2)}) collective-permute-start(f32[1,128,128]{2,1,0:T(8,128)S(1)} %get-tuple-element.12), channel_id=1, source_target_pairs={{0,1},{1,2},{2,3},{3,0},{4,5},{5,6},{6,7},{7,4},{8,9},{9,10},{10,1... | collective-permute-start | bytes 196616 | tf_op jit(solution)/shard_map/ppermute | solution.py:19
  601.0 9.1 %collective-permute-start.50 = (f32[1,128,128]{2,1,0:T(8,128)S(1)}, f32[1,128,128]{2,1,0:T(8,128)S(1)}, u32[]{:S(2)}, u32[]{:S(2)}) collective-permute-start(f32[1,128,128]{2,1,0:T(8,128)S(1)} %get-tuple-element.13), channel_id=1, source_target_pairs={{0,4},{4,8},{8,12},{12,0},{1,5},{5,9},{9,13},{13,1},{2,6},{6,10},{... | collective-permute-start | bytes 196616 | tf_op jit(solution)/shard_map/ppermute | solution.py:19
  601.0 9.1 %collective-permute-start.51 = (f32[1,128,128]{2,1,0:T(8,128)S(1)}, f32[1,128,128]{2,1,0:T(8,128)S(1)}, u32[]{:S(2)}, u32[]{:S(2)}) collective-permute-start(f32[1,128,128]{2,1,0:T(8,128)S(1)} %get-tuple-element.14), channel_id=1, source_target_pairs={{4,0},{8,4},{12,8},{0,12},{5,1},{9,5},{13,9},{1,13},{6,2},{10,6},{... | collective-permute-start | bytes 196616 | tf_op jit(solution)/shard_map/ppermute | solution.py:20
  (118 other events, 1049.8 us)
where the time goes:
time: 668 us; the launch traced here: 666 us
  blocking collectives  442 us (66%)
  other arithmetic  60.4 us (9%)
  starting transfers between devices  49.7 us (7%)
  waiting for transfers between devices  45.8 us (7%)
  matrix products  34.5 us (5%)
  local copies, waits for them, and re-layouts  29.8 us (4%)
    all_gather x5, blocking collectives, coarse_solve(): lax.all_gather(loads, ('gx', 'gy', 'gz'), axis=0, tiled=True)  192 us
    psum x3, blocking collectives, per_device(): lax.psum(jnp.stack([plus_inner(direction, image_now), plus_inner(directio...  127 us
    psum x3, blocking collectives, per_device(): totals = lax.psum(local_rows, ('gx', 'gy', 'gz'))  122 us
    unnamed x76, other arithmetic  32.8 us
    ppermute x27, starting transfers between devices, extended(): after = lax.ppermute(initial, axis, down)  29.9 us
    ppermute x27, waiting for transfers between devices, extended(): after = lax.ppermute(initial, axis, down)  28.2 us
    ppermute x27, starting transfers between devices, extended(): before = lax.ppermute(last, axis, up)  19.8 us
    ppermute x27, waiting for transfers between devices, extended(): before = lax.ppermute(last, axis, up)  17.5 us
  transfers between devices with their start and end apart: 54, of which 15 were waited for; matrix products, arithmetic and copies ran while one was open for 9% of the time, Pallas kernels for 0%

commit v1 on v0

--- a/solution.py
+++ b/solution.py
@@ -48,7 +48,14 @@
 
 def coarse_solve(loads, rows):
     return jnp.dot(
-        rows, lax.all_gather(loads, ("gx", "gy", "gz"), axis=0, tiled=True), precision=precise
+        rows,
+        jnp.concatenate(
+            lax.all_to_all(
+                jnp.stack([loads] * lax.axis_size(("gx", "gy", "gz"))), ("gx", "gy", "gz"), 0, 0
+            ),
+            axis=0,
+        ),
+        precision=precise,
     )
 
 

time: 668 us -> 510 us (0.76)
  blocking collectives: 442 us -> 248 us
  starting transfers between devices: 49.7 us -> 66.5 us
  waiting for transfers between devices: 45.8 us -> 62.3 us
  local copies, waits for them, and re-layouts: 29.8 us -> 37.1 us
    all_gather x5 -> x0, blocking collectives: 192 us -> none  [coarse_solve(): lax.all_gather(loads, ('gx', 'gy', 'gz'), axis=0, tiled=True)]
    all_to_all x0 -> x5, starting transfers between devices: none -> 30.3 us  [coarse_solve(): lax.all_to_all(jnp.stack([loads] * lax.axis_size(('gx', 'gy', 'gz'))), ('...]
    ppermute x27, starting transfers between devices: 29.9 us -> 15.8 us  [extended(): after = lax.ppermute(initial, axis, down)]
    ppermute x27, waiting for transfers between devices: 17.5 us -> 25.5 us  [extended(): before = lax.ppermute(last, axis, up)]
  transfers between devices with their start and end apart: 54 -> 59, of which waited for: 15 -> 24; matrix products, arithmetic and copies ran while one was open for 9% -> 11% of each run, Pallas kernels for 0% -> 0%
where the time goes in v1:
time: 510 us; the launch traced here: 508 us
  blocking collectives  248 us (49%)
  starting transfers between devices  66.5 us (13%)
  waiting for transfers between devices  62.3 us (12%)
  other arithmetic  54.3 us (11%)
  local copies, waits for them, and re-layouts  37.1 us (7%)
  matrix products  36.5 us (7%)
    psum x3, blocking collectives, per_device(): lax.psum(jnp.stack([plus_inner(direction, image_now), plus_inner(directio...  126 us
    psum x3, blocking collectives, per_device(): totals = lax.psum(local_rows, ('gx', 'gy', 'gz'))  122 us
    ppermute x27, waiting for transfers between devices, extended(): after = lax.ppermute(initial, axis, down)  30.9 us
    all_to_all x5, starting transfers between devices, coarse_solve(): lax.all_to_all(jnp.stack([loads] * lax.axis_size(('gx', 'gy', 'gz'))), ('...  30.3 us
    unnamed x76, other arithmetic  27.7 us
    ppermute x27, waiting for transfers between devices, extended(): before = lax.ppermute(last, axis, up)  25.5 us
    ppermute x27, starting transfers between devices, extended(): before = lax.ppermute(last, axis, up)  20.5 us
    ppermute x27, starting transfers between devices, extended(): after = lax.ppermute(initial, axis, down)  15.8 us
  transfers between devices with their start and end apart: 59, of which 24 were waited for; matrix products, arithmetic and copies ran while one was open for 11% of the time, Pallas kernels for 0%

profile of v1, /device:TPU:10, one launch (start us, length us, event | category | flops | bytes accessed | tf_op | source)
XLA Modules:
  0.0 507.6 jit_solution(14787604114004833429)
XLA Ops:
  2.1 6.0 %all-to-all-start = ((f32[32,6,128]{2,1,0:T(8,128)}), f32[32,6,128]{2,1,0:T(8,128)S(1)}, u32[]{:S(2)}, u32[]{:S(2)}) async-start(f32[32,6,128]{2,1,0:T(8,128)} %stack.164), calls=%async_computation | async-start | bytes 262144 | tf_op jit(solution)/shard_map/all_to_all | solution.py:53
  9.5 3.4 scatter_custom_fusion
  13.0 3.5 gather_fusion
  18.3 3.3 broadcast_select_fusion
  21.6 3.1 copy.28
  24.6 5.8 %gather_fusion.1 = f32[768,768]{1,0:T(8,128)} fusion(f32[768,768]{0,1:T(8,128)} %copy.28, s32[1024]{0:T(1024)S(1)} %pad_clamp_fusion), kind=kCustom, calls=%fused_computation.1 | custom fusion | bytes 4721664 | tf_op jit(solution)/shard_map/jit(_take)/gather | solution.py:88
  32.5 3.3 select_bitcast_fusion
  35.9 3.1 copy.29
  47.6 3.7 fusion.4
  52.0 3.7 collective-permute-done.6
  58.9 3.7 collective-permute-done.7
  65.0 5.4 %all-to-all-start.1 = ((f32[32,6,128]{2,1,0:T(8,128)}), f32[32,6,128]{2,1,0:T(8,128)S(1)}, u32[]{:S(2)}, u32[]{:S(2)}) async-start(f32[32,6,128]{2,1,0:T(8,128)} %stack.167), calls=%async_computation.1 | async-start | bytes 262144 | tf_op jit(solution)/shard_map/all_to_all | solution.py:53
  72.2 4.1 all-to-all-done.1
  91.1 43.5 %psum.42 = f32[40,128]{1,0:T(8,128)} all-reduce(f32[40,128]{1,0:T(8,128)S(1)} %convolution_bitcast_fusion.5), channel_id=1, replica_groups=mesh['gx'=2,'gy'=4,'gz'=4] {'gx','gy','gz'}, use_global_device_ids=true, to_apply=%region_1.2 | all-reduce | flops 5120 | bytes 40960 | tf_op jit(solution)/shard_map/psum | solution.py:110
  136.5 3.7 convolution_multiply_fusion.2
  140.4 4.1 collective-permute-done.18
  147.8 3.7 collective-permute-done.19
  152.9 5.0 all-to-all-start.2
  176.8 2.9 collective-permute-done.25
  182.9 41.5 %psum.43 = f32[2,128]{1,0:T(2,128)S(1)} all-reduce(f32[2,128]{1,0:T(2,128)S(1)} %pad_maximum_fusion.2), channel_id=1, replica_groups=mesh['gx'=2,'gy'=4,'gz'=4] {'gx','gy','gz'}, use_global_device_ids=true, to_apply=%region_4.5 | all-reduce | flops 256 | bytes 2048 | tf_op jit(solution)/shard_map/psum | solution.py:116
  228.2 39.0 %psum.44 = f32[41,128]{1,0:T(8,128)S(1)} all-reduce(f32[41,128]{1,0:T(8,128)S(1)} %pad_maximum_fusion), channel_id=1, replica_groups=mesh['gx'=2,'gy'=4,'gz'=4] {'gx','gy','gz'}, use_global_device_ids=true, to_apply=%region_6.7 | all-reduce | flops 5248 | bytes 41984 | tf_op jit(solution)/shard_map/psum | solution.py:110
  270.4 3.7 convolution_multiply_fusion.1
  274.4 4.1 collective-permute-done.30
  281.8 3.9 collective-permute-done.31
  287.3 6.9 %all-to-all-start.3 = ((f32[32,6,128]{2,1,0:T(8,128)}), f32[32,6,128]{2,1,0:T(8,128)}, u32[]{:S(2)}, u32[]{:S(2)}) async-start(f32[32,6,128]{2,1,0:T(8,128)} %stack.177), calls=%async_computation.3 | async-start | bytes 262144 | tf_op jit(solution)/shard_map/all_to_all | solution.py:53
  319.7 41.7 %psum.45 = f32[2,128]{1,0:T(2,128)} all-reduce(f32[2,128]{1,0:T(2,128)} %pad_maximum_fusion.3), channel_id=1, replica_groups=mesh['gx'=2,'gy'=4,'gz'=4] {'gx','gy','gz'}, use_global_device_ids=true, to_apply=%region_9.10 | all-reduce | flops 256 | bytes 2048 | tf_op jit(solution)/shard_map/psum | solution.py:116
  365.5 39.2 %psum.46 = f32[42,128]{1,0:T(8,128)S(1)} all-reduce(f32[42,128]{1,0:T(8,128)S(1)} %pad_maximum_fusion.1), channel_id=1, replica_groups=mesh['gx'=2,'gy'=4,'gz'=4] {'gx','gy','gz'}, use_global_device_ids=true, to_apply=%region_12.13 | all-reduce | flops 5376 | bytes 43008 | tf_op jit(solution)/shard_map/psum | solution.py:110
  408.2 3.7 convolution_multiply_fusion
  412.2 4.1 collective-permute-done.42
  419.6 3.9 collective-permute-done.43
  425.1 6.9 %all-to-all-start.4 = ((f32[32,6,128]{2,1,0:T(8,128)}), f32[32,6,128]{2,1,0:T(8,128)}, u32[]{:S(2)}, u32[]{:S(2)}) async-start(f32[32,6,128]{2,1,0:T(8,128)} %stack.185), calls=%async_computation.4 | async-start | bytes 262144 | tf_op jit(solution)/shard_map/all_to_all | solution.py:53
  455.1 42.9 %psum.47 = f32[2,128]{1,0:T(2,128)S(1)} all-reduce(f32[2,128]{1,0:T(2,128)S(1)} %pad_maximum_fusion.4), channel_id=1, replica_groups=mesh['gx'=2,'gy'=4,'gz'=4] {'gx','gy','gz'}, use_global_device_ids=true, to_apply=%region_15.16 | all-reduce | flops 256 | bytes 2048 | tf_op jit(solution)/shard_map/psum | solution.py:116
  (460 shorter events, 148.0 us)
Async XLA Ops:
  2.1 14.4 %all-to-all-start = ((f32[32,6,128]{2,1,0:T(8,128)}), f32[32,6,128]{2,1,0:T(8,128)S(1)}, u32[]{:S(2)}, u32[]{:S(2)}) async-start(f32[32,6,128]{2,1,0:T(8,128)} %stack.164), calls=%async_computation | async-start | bytes 262144 | tf_op jit(solution)/shard_map/all_to_all | solution.py:53
  17.6 12.8 %collective-permute-start = (f32[1,128,128]{2,1,0:T(8,128)S(1)}, f32[1,128,128]{2,1,0:T(8,128)S(1)}, u32[]{:S(2)}, u32[]{:S(2)}) collective-permute-start(f32[1,128,128]{2,1,0:T(8,128)S(1)} %slice.456), channel_id=1, source_target_pairs={{0,16},{16,0},{1,17},{17,1},{2,18},{18,2},{3,19},{19,3},{4,20},{20... | collective-permute-start | bytes 196616 | tf_op jit(solution)/shard_map/ppermute | solution.py:19
  31.1 10.5 %collective-permute-start.1 = (f32[1,128,128]{2,1,0:T(8,128)}, f32[1,128,128]{2,1,0:T(8,128)}, u32[]{:S(2)}, u32[]{:S(2)}) collective-permute-start(f32[1,128,128]{2,1,0:T(8,128)} %get-tuple-element.63), channel_id=1, source_target_pairs={{16,0},{0,16},{17,1},{1,17},{18,2},{2,18},{19,3},{3,19},{20,4},{4,... | collective-permute-start | bytes 196616 | tf_op jit(solution)/shard_map/ppermute | solution.py:20
  38.9 7.9 %collective-permute-start.5 = (f32[1,128,128]{2,1,0:T(8,128)S(1)}, f32[1,128,128]{2,1,0:T(8,128)S(1)}, u32[]{:S(2)}, u32[]{:S(2)}) collective-permute-start(f32[1,128,128]{2,1,0:T(8,128)S(1)} %get-tuple-element.58), channel_id=1, source_target_pairs={{1,0},{2,1},{3,2},{0,3},{5,4},{6,5},{7,6},{4,7},{9,8},{10,9},{11,1... | collective-permute-start | bytes 196616 | tf_op jit(solution)/shard_map/ppermute | solution.py:20
  39.5 7.3 %collective-permute-start.4 = (f32[1,128,128]{2,1,0:T(8,128)S(1)}, f32[1,128,128]{2,1,0:T(8,128)S(1)}, u32[]{:S(2)}, u32[]{:S(2)}) collective-permute-start(f32[1,128,128]{2,1,0:T(8,128)S(1)} %get-tuple-element.60), channel_id=1, source_target_pairs={{0,1},{1,2},{2,3},{3,0},{4,5},{5,6},{6,7},{7,4},{8,9},{9,10},{10,1... | collective-permute-start | bytes 196616 | tf_op jit(solution)/shard_map/ppermute | solution.py:19
  55.7 7.6 %collective-permute-start.11 = (f32[1,128,128]{2,1,0:T(8,128)S(1)}, f32[1,128,128]{2,1,0:T(8,128)S(1)}, u32[]{:S(2)}, u32[]{:S(2)}) collective-permute-start(f32[1,128,128]{2,1,0:T(8,128)S(1)} %get-tuple-element.52), channel_id=1, source_target_pairs={{1,0},{2,1},{3,2},{0,3},{5,4},{6,5},{7,6},{4,7},{9,8},{10,9},{11,1... | collective-permute-start | bytes 196616 | tf_op jit(solution)/shard_map/ppermute | solution.py:20
  55.8 7.5 %collective-permute-start.10 = (f32[1,128,128]{2,1,0:T(8,128)S(1)}, f32[1,128,128]{2,1,0:T(8,128)S(1)}, u32[]{:S(2)}, u32[]{:S(2)}) collective-permute-start(f32[1,128,128]{2,1,0:T(8,128)S(1)} %get-tuple-element.54), channel_id=1, source_target_pairs={{0,1},{1,2},{2,3},{3,0},{4,5},{5,6},{6,7},{7,4},{8,9},{9,10},{10,1... | collective-permute-start | bytes 196616 | tf_op jit(solution)/shard_map/ppermute | solution.py:19
  56.3 6.3 %collective-permute-start.8 = (f32[1,128,128]{2,1,0:T(8,128)S(1)}, f32[1,128,128]{2,1,0:T(8,128)S(1)}, u32[]{:S(2)}, u32[]{:S(2)}) collective-permute-start(f32[1,128,128]{2,1,0:T(8,128)S(1)} %get-tuple-element.55), channel_id=1, source_target_pairs={{0,4},{4,8},{8,12},{12,0},{1,5},{5,9},{9,13},{13,1},{2,6},{6,10},{... | collective-permute-start | bytes 196616 | tf_op jit(solution)/shard_map/ppermute | solution.py:19
  56.8 6.4 %collective-permute-start.9 = (f32[1,128,128]{2,1,0:T(8,128)S(1)}, f32[1,128,128]{2,1,0:T(8,128)S(1)}, u32[]{:S(2)}, u32[]{:S(2)}) collective-permute-start(f32[1,128,128]{2,1,0:T(8,128)S(1)} %get-tuple-element.56), channel_id=1, source_target_pairs={{4,0},{8,4},{12,8},{0,12},{5,1},{9,5},{13,9},{1,13},{6,2},{10,6},{... | collective-permute-start | bytes 196616 | tf_op jit(solution)/shard_map/ppermute | solution.py:20
  65.0 11.3 %all-to-all-start.1 = ((f32[32,6,128]{2,1,0:T(8,128)}), f32[32,6,128]{2,1,0:T(8,128)S(1)}, u32[]{:S(2)}, u32[]{:S(2)}) async-start(f32[32,6,128]{2,1,0:T(8,128)} %stack.167), calls=%async_computation.1 | async-start | bytes 262144 | tf_op jit(solution)/shard_map/all_to_all | solution.py:53
  81.8 7.0 %collective-permute-start.17 = (f32[1,128,128]{2,1,0:T(8,128)S(1)}, f32[1,128,128]{2,1,0:T(8,128)S(1)}, u32[]{:S(2)}, u32[]{:S(2)}) collective-permute-start(f32[1,128,128]{2,1,0:T(8,128)S(1)} %get-tuple-element.46), channel_id=1, source_target_pairs={{1,0},{2,1},{3,2},{0,3},{5,4},{6,5},{7,6},{4,7},{9,8},{10,9},{11,1... | collective-permute-start | bytes 196616 | tf_op jit(solution)/shard_map/ppermute | solution.py:20
  81.8 6.9 %collective-permute-start.16 = (f32[1,128,128]{2,1,0:T(8,128)S(1)}, f32[1,128,128]{2,1,0:T(8,128)S(1)}, u32[]{:S(2)}, u32[]{:S(2)}) collective-permute-start(f32[1,128,128]{2,1,0:T(8,128)S(1)} %get-tuple-element.48), channel_id=1, source_target_pairs={{0,1},{1,2},{2,3},{3,0},{4,5},{5,6},{6,7},{7,4},{8,9},{9,10},{10,1... | collective-permute-start | bytes 196616 | tf_op jit(solution)/shard_map/ppermute | solution.py:19
  144.6 7.1 %collective-permute-start.23 = (f32[1,128,128]{2,1,0:T(8,128)S(1)}, f32[1,128,128]{2,1,0:T(8,128)S(1)}, u32[]{:S(2)}, u32[]{:S(2)}) collective-permute-start(f32[1,128,128]{2,1,0:T(8,128)S(1)} %get-tuple-element.40), channel_id=1, source_target_pairs={{1,0},{2,1},{3,2},{0,3},{5,4},{6,5},{7,6},{4,7},{9,8},{10,9},{11,1... | collective-permute-start | bytes 196616 | tf_op jit(solution)/shard_map/ppermute | solution.py:20
  144.6 7.0 %collective-permute-start.22 = (f32[1,128,128]{2,1,0:T(8,128)S(1)}, f32[1,128,128]{2,1,0:T(8,128)S(1)}, u32[]{:S(2)}, u32[]{:S(2)}) collective-permute-start(f32[1,128,128]{2,1,0:T(8,128)S(1)} %get-tuple-element.42), channel_id=1, source_target_pairs={{0,1},{1,2},{2,3},{3,0},{4,5},{5,6},{6,7},{7,4},{8,9},{9,10},{10,1... | collective-permute-start | bytes 196616 | tf_op jit(solution)/shard_map/ppermute | solution.py:19
  145.1 6.4 %collective-permute-start.20 = (f32[1,128,128]{2,1,0:T(8,128)S(1)}, f32[1,128,128]{2,1,0:T(8,128)S(1)}, u32[]{:S(2)}, u32[]{:S(2)}) collective-permute-start(f32[1,128,128]{2,1,0:T(8,128)S(1)} %get-tuple-element.43), channel_id=1, source_target_pairs={{0,4},{4,8},{8,12},{12,0},{1,5},{5,9},{9,13},{13,1},{2,6},{6,10},{... | collective-permute-start | bytes 196616 | tf_op jit(solution)/shard_map/ppermute | solution.py:19
  152.9 11.0 %all-to-all-start.2 = ((f32[32,6,128]{2,1,0:T(8,128)}), f32[32,6,128]{2,1,0:T(8,128)}, u32[]{:S(2)}, u32[]{:S(2)}) async-start(f32[32,6,128]{2,1,0:T(8,128)} %stack.170), calls=%async_computation.2 | async-start | bytes 262144 | tf_op jit(solution)/shard_map/all_to_all | solution.py:53
  172.5 8.3 %collective-permute-start.29 = (f32[1,128,128]{2,1,0:T(8,128)S(1)}, f32[1,128,128]{2,1,0:T(8,128)S(1)}, u32[]{:S(2)}, u32[]{:S(2)}) collective-permute-start(f32[1,128,128]{2,1,0:T(8,128)S(1)} %get-tuple-element.34), channel_id=1, source_target_pairs={{1,0},{2,1},{3,2},{0,3},{5,4},{6,5},{7,6},{4,7},{9,8},{10,9},{11,1... | collective-permute-start | bytes 196616 | tf_op jit(solution)/shard_map/ppermute | solution.py:20
  172.6 8.2 %collective-permute-start.28 = (f32[1,128,128]{2,1,0:T(8,128)S(1)}, f32[1,128,128]{2,1,0:T(8,128)S(1)}, u32[]{:S(2)}, u32[]{:S(2)}) collective-permute-start(f32[1,128,128]{2,1,0:T(8,128)S(1)} %get-tuple-element.36), channel_id=1, source_target_pairs={{0,1},{1,2},{2,3},{3,0},{4,5},{5,6},{6,7},{7,4},{8,9},{9,10},{10,1... | collective-permute-start | bytes 196616 | tf_op jit(solution)/shard_map/ppermute | solution.py:19
  173.1 6.6 %collective-permute-start.26 = (f32[1,128,128]{2,1,0:T(8,128)S(1)}, f32[1,128,128]{2,1,0:T(8,128)S(1)}, u32[]{:S(2)}, u32[]{:S(2)}) collective-permute-start(f32[1,128,128]{2,1,0:T(8,128)S(1)} %get-tuple-element.37), channel_id=1, source_target_pairs={{0,4},{4,8},{8,12},{12,0},{1,5},{5,9},{9,13},{13,1},{2,6},{6,10},{... | collective-permute-start | bytes 196616 | tf_op jit(solution)/shard_map/ppermute | solution.py:19
  278.5 7.4 %collective-permute-start.35 = (f32[1,128,128]{2,1,0:T(8,128)S(1)}, f32[1,128,128]{2,1,0:T(8,128)S(1)}, u32[]{:S(2)}, u32[]{:S(2)}) collective-permute-start(f32[1,128,128]{2,1,0:T(8,128)S(1)} %get-tuple-element.28), channel_id=1, source_target_pairs={{1,0},{2,1},{3,2},{0,3},{5,4},{6,5},{7,6},{4,7},{9,8},{10,9},{11,1... | collective-permute-start | bytes 196616 | tf_op jit(solution)/shard_map/ppermute | solution.py:20
  278.5 7.3 %collective-permute-start.34 = (f32[1,128,128]{2,1,0:T(8,128)S(1)}, f32[1,128,128]{2,1,0:T(8,128)S(1)}, u32[]{:S(2)}, u32[]{:S(2)}) collective-permute-start(f32[1,128,128]{2,1,0:T(8,128)S(1)} %get-tuple-element.30), channel_id=1, source_target_pairs={{0,1},{1,2},{2,3},{3,0},{4,5},{5,6},{6,7},{7,4},{8,9},{9,10},{10,1... | collective-permute-start | bytes 196616 | tf_op jit(solution)/shard_map/ppermute | solution.py:19
  279.0 6.7 %collective-permute-start.32 = (f32[1,128,128]{2,1,0:T(8,128)S(1)}, f32[1,128,128]{2,1,0:T(8,128)S(1)}, u32[]{:S(2)}, u32[]{:S(2)}) collective-permute-start(f32[1,128,128]{2,1,0:T(8,128)S(1)} %get-tuple-element.31), channel_id=1, source_target_pairs={{0,4},{4,8},{8,12},{12,0},{1,5},{5,9},{9,13},{13,1},{2,6},{6,10},{... | collective-permute-start | bytes 196616 | tf_op jit(solution)/shard_map/ppermute | solution.py:19
  287.3 12.9 %all-to-all-start.3 = ((f32[32,6,128]{2,1,0:T(8,128)}), f32[32,6,128]{2,1,0:T(8,128)}, u32[]{:S(2)}, u32[]{:S(2)}) async-start(f32[32,6,128]{2,1,0:T(8,128)} %stack.177), calls=%async_computation.3 | async-start | bytes 262144 | tf_op jit(solution)/shard_map/all_to_all | solution.py:53
  308.8 8.3 %collective-permute-start.41 = (f32[1,128,128]{2,1,0:T(8,128)S(1)}, f32[1,128,128]{2,1,0:T(8,128)S(1)}, u32[]{:S(2)}, u32[]{:S(2)}) collective-permute-start(f32[1,128,128]{2,1,0:T(8,128)S(1)} %get-tuple-element.22), channel_id=1, source_target_pairs={{1,0},{2,1},{3,2},{0,3},{5,4},{6,5},{7,6},{4,7},{9,8},{10,9},{11,1... | collective-permute-start | bytes 196616 | tf_op jit(solution)/shard_map/ppermute | solution.py:20
  308.8 8.2 %collective-permute-start.40 = (f32[1,128,128]{2,1,0:T(8,128)S(1)}, f32[1,128,128]{2,1,0:T(8,128)S(1)}, u32[]{:S(2)}, u32[]{:S(2)}) collective-permute-start(f32[1,128,128]{2,1,0:T(8,128)S(1)} %get-tuple-element.24), channel_id=1, source_target_pairs={{0,1},{1,2},{2,3},{3,0},{4,5},{5,6},{6,7},{7,4},{8,9},{9,10},{10,1... | collective-permute-start | bytes 196616 | tf_op jit(solution)/shard_map/ppermute | solution.py:19
  309.3 6.6 %collective-permute-start.38 = (f32[1,128,128]{2,1,0:T(8,128)S(1)}, f32[1,128,128]{2,1,0:T(8,128)S(1)}, u32[]{:S(2)}, u32[]{:S(2)}) collective-permute-start(f32[1,128,128]{2,1,0:T(8,128)S(1)} %get-tuple-element.25), channel_id=1, source_target_pairs={{0,4},{4,8},{8,12},{12,0},{1,5},{5,9},{9,13},{13,1},{2,6},{6,10},{... | collective-permute-start | bytes 196616 | tf_op jit(solution)/shard_map/ppermute | solution.py:19
  416.3 7.3 %collective-permute-start.47 = (f32[1,128,128]{2,1,0:T(8,128)S(1)}, f32[1,128,128]{2,1,0:T(8,128)S(1)}, u32[]{:S(2)}, u32[]{:S(2)}) collective-permute-start(f32[1,128,128]{2,1,0:T(8,128)S(1)} %get-tuple-element.16), channel_id=1, source_target_pairs={{1,0},{2,1},{3,2},{0,3},{5,4},{6,5},{7,6},{4,7},{9,8},{10,9},{11,1... | collective-permute-start | bytes 196616 | tf_op jit(solution)/shard_map/ppermute | solution.py:20
  416.4 7.2 %collective-permute-start.46 = (f32[1,128,128]{2,1,0:T(8,128)S(1)}, f32[1,128,128]{2,1,0:T(8,128)S(1)}, u32[]{:S(2)}, u32[]{:S(2)}) collective-permute-start(f32[1,128,128]{2,1,0:T(8,128)S(1)} %get-tuple-element.18), channel_id=1, source_target_pairs={{0,1},{1,2},{2,3},{3,0},{4,5},{5,6},{6,7},{7,4},{8,9},{9,10},{10,1... | collective-permute-start | bytes 196616 | tf_op jit(solution)/shard_map/ppermute | solution.py:19
  416.9 6.7 %collective-permute-start.44 = (f32[1,128,128]{2,1,0:T(8,128)S(1)}, f32[1,128,128]{2,1,0:T(8,128)S(1)}, u32[]{:S(2)}, u32[]{:S(2)}) collective-permute-start(f32[1,128,128]{2,1,0:T(8,128)S(1)} %get-tuple-element.19), channel_id=1, source_target_pairs={{0,4},{4,8},{8,12},{12,0},{1,5},{5,9},{9,13},{13,1},{2,6},{6,10},{... | collective-permute-start | bytes 196616 | tf_op jit(solution)/shard_map/ppermute | solution.py:19
  425.1 12.9 %all-to-all-start.4 = ((f32[32,6,128]{2,1,0:T(8,128)}), f32[32,6,128]{2,1,0:T(8,128)}, u32[]{:S(2)}, u32[]{:S(2)}) async-start(f32[32,6,128]{2,1,0:T(8,128)} %stack.185), calls=%async_computation.4 | async-start | bytes 262144 | tf_op jit(solution)/shard_map/all_to_all | solution.py:53
  446.7 7.0 %collective-permute-start.53 = (f32[1,128,128]{2,1,0:T(8,128)S(1)}, f32[1,128,128]{2,1,0:T(8,128)S(1)}, u32[]{:S(2)}, u32[]{:S(2)}) collective-permute-start(f32[1,128,128]{2,1,0:T(8,128)S(1)} %get-tuple-element.10), channel_id=1, source_target_pairs={{1,0},{2,1},{3,2},{0,3},{5,4},{6,5},{7,6},{4,7},{9,8},{10,9},{11,1... | collective-permute-start | bytes 196616 | tf_op jit(solution)/shard_map/ppermute | solution.py:20
  446.7 6.9 %collective-permute-start.52 = (f32[1,128,128]{2,1,0:T(8,128)S(1)}, f32[1,128,128]{2,1,0:T(8,128)S(1)}, u32[]{:S(2)}, u32[]{:S(2)}) collective-permute-start(f32[1,128,128]{2,1,0:T(8,128)S(1)} %get-tuple-element.12), channel_id=1, source_target_pairs={{0,1},{1,2},{2,3},{3,0},{4,5},{5,6},{6,7},{7,4},{8,9},{9,10},{10,1... | collective-permute-start | bytes 196616 | tf_op jit(solution)/shard_map/ppermute | solution.py:19
  (119 other events, 949.2 us)
